TPU v7x, 32 devices: a whole 2x2x4 slice. The times are simulated.
32 devices in a mesh: cell: 2 (over x), ap: 8 (over z, y), sc: 2 (over core).
Axes of the slice: x: 2, y: 2, z: 4, core: 2. Of those that a mesh axis runs over, the one named last changes fastest.
Arguments:
- unsmoothed_link_guesses: bfloat16 [32, 4, 2, 128, 2048], P(('cell', 'ap'), None, None, None, 'sc'), parts along dimension 0, may hold values from -24 to 24
- received: bfloat16 [32, 4, 2, 4, 2048], P(('cell', 'ap'), None, None, None, 'sc'), parts along dimension 0, may hold values from -6 to 6
- user_power: float32 [256], P('cell'), parts along dimension 0, may hold values from 0.25 to 4
- noise_power: float32 [32], P(('cell', 'ap')), parts along dimension 0, may hold values from 0.1 to 1
- ap_gain: float32 [32, 128], P(('cell', 'ap')), parts along dimension 0, may hold values from 0.5 to 4
- user_cluster: int32 [256], P('cell'), parts along dimension 0, may hold values from 0 to 15, as said below
- serving: int32 [32, 16], P('cell'), parts along dimension 0, may hold values from 0 to 1, as said below
- cluster_owner: int32 [32, 1], P('cell'), parts along dimension 0, may hold values from 0 to 7, as said below
Outputs:
- estimates: float32 [64, 8, 4, 2, 2048], P(('cell', 'ap'), None, None, None, 'sc'), parts along dimension 0
There are 2 independent parts, one for each index of `cell`. A program takes and returns all parts, laid end to end along the dimension named above; each array names one. Nothing has to cross between parts.
Inputs may be any that keep to these rules, and one draw needn't show every extreme that they name: `user_cluster`: each of the 16 clusters holds exactly 8 users. `serving`: column a belongs to index a // 2 of ap. Where a cluster is served by an index of ap, at least one of its access points serves it. Of the clusters that one index of ap serves, at most 2 have the same owner; in every draw some owner has exactly 2 of its clusters served by every index of ap. `cluster_owner`: at most 4 clusters have the same owner, and some owner has exactly 4.
All inputs are finite; a program needn't handle non-finite values.
Results may differ from a plain program's by a relative error of at most 0.017.
Values may be sent and summed in bfloat16 or wider, within the bound.
A program may use at most 128 MiB of HBM per device.

v0:
```python
import math
import jax
import jax.numpy as jnp
from jax import lax
from jax.sharding import PartitionSpec as P

TONE_NUMBER = 2048
TAPS = 64
CU = 8
OWN_MAX = 4


def complex_times(left_factor, right_factor):
    return (
        left_factor[0] * right_factor[0] - left_factor[1] * right_factor[1],
        left_factor[0] * right_factor[1] + left_factor[1] * right_factor[0],
    )


def times_conj(left_factor, right_factor):
    return (
        left_factor[0] * right_factor[0] + left_factor[1] * right_factor[1],
        left_factor[1] * right_factor[0] - left_factor[0] * right_factor[1],
    )


def hermitian_solve(cov_re, cov_im, right_re, right_im):
    dimension = len(cov_re)
    factor = {}
    pivots = []
    for j in range(dimension):
        pivot_root = cov_re[j][j]
        for k in range(j):
            element = factor[j, k]
            pivot_root = pivot_root - (element[0] * element[0] + element[1] * element[1])
        pivot_root = jnp.sqrt(pivot_root)
        pivots.append(pivot_root)
        for i in range(j + 1, dimension):
            running = (cov_re[i][j], cov_im[i][j])
            for k in range(j):
                product = times_conj(factor[i, k], factor[j, k])
                running = (running[0] - product[0], running[1] - product[1])
            factor[i, j] = (running[0] / pivot_root, running[1] / pivot_root)
    forward = []
    for i in range(dimension):
        running = (right_re[i], right_im[i])
        for k in range(i):
            product = complex_times(factor[i, k], forward[k])
            running = (running[0] - product[0], running[1] - product[1])
        forward.append((running[0] / pivots[i], running[1] / pivots[i]))
    result = [None] * dimension
    for i in range(dimension - 1, -1, -1):
        running = forward[i]
        for k in range(i + 1, dimension):
            product = times_conj(result[k], factor[k, i])
            running = (running[0] - product[0], running[1] - product[1])
        result[i] = (running[0] / pivots[i], running[1] / pivots[i])
    return result


def tone_angles(lowest_tone, tone_quantity, tones_first):
    if tones_first:
        tone_values = lowest_tone + lax.broadcasted_iota(jnp.int32, (tone_quantity, TAPS), 0)
        lag_values = lax.broadcasted_iota(jnp.int32, (tone_quantity, TAPS), 1)
    else:
        tone_values = lowest_tone + lax.broadcasted_iota(jnp.int32, (TAPS, tone_quantity), 1)
        lag_values = lax.broadcasted_iota(jnp.int32, (TAPS, tone_quantity), 0)
    rotation = tone_values * lag_values % TONE_NUMBER
    return rotation.astype(jnp.float32) * (2.0 * math.pi / TONE_NUMBER)


def forward_table(lowest_tone, tone_quantity):
    angles = tone_angles(lowest_tone, tone_quantity, True)
    return jnp.concatenate([jnp.cos(angles), jnp.sin(angles)], axis=1).astype(jnp.bfloat16)


def rebuild_tables(lowest_tone, tone_quantity):
    angles = tone_angles(lowest_tone, tone_quantity, False)
    cosine = jnp.cos(angles).astype(jnp.bfloat16)
    sine = jnp.sin(angles).astype(jnp.bfloat16)
    return (jnp.concatenate([cosine, sine], axis=0), jnp.concatenate([-sine, cosine], axis=0))


def rotate_matrix():
    rows = lax.broadcasted_iota(jnp.int32, (2 * TAPS, 2 * TAPS), 0)
    cols = lax.broadcasted_iota(jnp.int32, (2 * TAPS, 2 * TAPS), 1)
    lower = jnp.where((cols < TAPS) & (rows == cols + TAPS), -1.0, 0.0)
    upper = jnp.where((cols >= TAPS) & (rows == cols - TAPS), 1.0, 0.0)
    return (lower + upper).astype(jnp.float32)


def local_estimates(smooth_re, smooth_im, power_row, noise_level, right_side, weight_row):
    antennas = smooth_re.shape[0]
    user_scale = (power_row / smooth_re.shape[1])[:, None]
    scaled_re = [smooth_re[i] * user_scale for i in range(antennas)]
    scaled_im = [smooth_im[i] * user_scale for i in range(antennas)]
    cov_re = [[None] * antennas for i in range(antennas)]
    cov_im = [[None] * antennas for i in range(antennas)]
    for i in range(antennas):
        for j in range(i + 1):
            cov_re[i][j] = jnp.sum(
                scaled_re[i] * smooth_re[j] + scaled_im[i] * smooth_im[j], axis=0
            )
            if i == j:
                cov_re[i][j] = cov_re[i][j] + noise_level
            else:
                cov_im[i][j] = jnp.sum(
                    scaled_im[i] * smooth_re[j] - scaled_re[i] * smooth_im[j], axis=0
                )
    signal = right_side.astype(jnp.float32)
    solved = hermitian_solve(cov_re, cov_im, signal[:, 0], signal[:, 1])
    est_re = (
        smooth_re[0][:, None, :] * solved[0][0][None]
        + smooth_im[0][:, None, :] * solved[0][1][None]
    )
    est_im = (
        smooth_re[0][:, None, :] * solved[0][1][None]
        - smooth_im[0][:, None, :] * solved[0][0][None]
    )
    for i in range(1, antennas):
        est_re = (
            est_re
            + smooth_re[i][:, None, :] * solved[i][0][None]
            + smooth_im[i][:, None, :] * solved[i][1][None]
        )
        est_im = (
            est_im
            + smooth_re[i][:, None, :] * solved[i][1][None]
            - smooth_im[i][:, None, :] * solved[i][0][None]
        )
    return weight_row[:, None, None, None] * jnp.stack([est_re, est_im], axis=2)


def local(
    unsmoothed_link_guesses,
    received,
    user_power,
    noise_power,
    ap_gain,
    user_cluster,
    serving,
    cluster_owner,
):
    ap_count = unsmoothed_link_guesses.shape[0]
    antennas = unsmoothed_link_guesses.shape[1]
    user_count = unsmoothed_link_guesses.shape[3]
    tone_positions = unsmoothed_link_guesses.shape[4]
    clusters = serving.shape[0]
    devices = lax.axis_size("ap")
    device = lax.axis_index("ap")
    lowest_tone = lax.axis_index("sc") * tone_positions
    products = jnp.dot(
        unsmoothed_link_guesses.reshape(-1, tone_positions),
        forward_table(lowest_tone, tone_positions),
        preferred_element_type=jnp.float32,
    )
    products = products.reshape((ap_count, antennas, 2, user_count, 2 * TAPS))
    rotated = jnp.dot(
        products[:, :, 1].reshape(-1, 2 * TAPS), rotate_matrix(), precision=lax.Precision.HIGHEST
    )
    combined = (
        products[:, :, 0] + rotated.reshape((ap_count, antennas, user_count, 2 * TAPS))
    ) / TONE_NUMBER
    coefficients = lax.psum(combined.astype(jnp.bfloat16), "sc")
    coef_b = coefficients.reshape(-1, 2 * TAPS)
    table_re, table_im = rebuild_tables(lowest_tone, tone_positions)
    smooth_re = jnp.dot(coef_b, table_re, preferred_element_type=jnp.float32).reshape(
        (ap_count, antennas, user_count, tone_positions)
    )
    smooth_im = jnp.dot(coef_b, table_im, preferred_element_type=jnp.float32).reshape(
        (ap_count, antennas, user_count, tone_positions)
    )
    cluster_ids = jnp.arange(clusters, dtype=jnp.int32)
    onehot = (user_cluster[:, None] == cluster_ids[None, :]).astype(jnp.float32)
    own_columns = lax.dynamic_slice_in_dim(serving, device * ap_count, ap_count, 1).astype(
        jnp.float32
    )
    weights = jnp.dot(onehot, own_columns, precision=lax.Precision.HIGHEST).T * ap_gain
    totals = lax.psum(jnp.sum(weights, axis=0), "ap")
    partial_value = local_estimates(
        smooth_re[0], smooth_im[0], user_power, noise_power[0], received[0], weights[0]
    )
    partial_value = partial_value + local_estimates(
        smooth_re[1], smooth_im[1], user_power, noise_power[1], received[1], weights[1]
    )
    partial_value = partial_value.astype(jnp.bfloat16)
    owner_map = cluster_owner[:, 0]
    same_owner = owner_map[:, None] == owner_map[None, :]
    earlier = cluster_ids[None, :] < cluster_ids[:, None]
    cluster_rank = jnp.sum(same_owner & earlier, axis=1)
    user_ids = jnp.arange(user_count, dtype=jnp.int32)
    position = jnp.sum(
        (user_cluster[:, None] == user_cluster[None, :]) & (user_ids[None, :] < user_ids[:, None]),
        axis=1,
    )
    member_hits = (user_cluster[None, None, :] == cluster_ids[:, None, None]) & (
        position[None, None, :] == jnp.arange(CU, dtype=jnp.int32)[None, :, None]
    )
    members = jnp.sum(jnp.where(member_hits, user_ids[None, None, :], 0), axis=2)
    slot_ids = jnp.arange(devices * OWN_MAX, dtype=jnp.int32)
    slot_hits = (owner_map[None, :] == (slot_ids // OWN_MAX)[:, None]) & (
        cluster_rank[None, :] == (slot_ids % OWN_MAX)[:, None]
    )
    hit_table = slot_hits.astype(jnp.int32)
    filled = jnp.sum(hit_table, axis=1)
    member_rows = jnp.sum(hit_table[:, :, None] * members[None], axis=1)
    picked = jnp.take(partial_value, member_rows.reshape(-1), axis=0)
    picked = picked.reshape(member_rows.shape + partial_value.shape[1:])
    owner_sums = lax.psum_scatter(
        picked * filled.astype(jnp.bfloat16)[:, None, None, None, None],
        "ap",
        scatter_dimension=0,
        tiled=True,
    ).astype(jnp.float32)
    my_hits = (
        (owner_map[None, :] == device)
        & (cluster_rank[None, :] == jnp.arange(OWN_MAX, dtype=jnp.int32)[:, None])
    ).astype(jnp.int32)
    my_rows = jnp.sum(my_hits[:, :, None] * members[None], axis=1)
    my_filled = jnp.sum(my_hits, axis=1).astype(jnp.float32)
    denominator = (
        1.0 + jnp.take(totals, my_rows.reshape(-1)).reshape(my_rows.shape) * my_filled[:, None]
    )
    return owner_sums / denominator[:, :, None, None, None]


def solution(mesh):
    placed = (
        P(("cell", "ap"), None, None, None, "sc"),
        P(("cell", "ap"), None, None, None, "sc"),
        P("cell"),
        P(("cell", "ap")),
        P(("cell", "ap"), None),
        P("cell"),
        P("cell", None),
        P("cell", None),
    )
    return jax.shard_map(
        local,
        mesh=mesh,
        in_specs=placed,
        out_specs=P(("cell", "ap"), None, None, None, "sc"),
        check_vma=False,
    )
```

profile of v0, /device:TPU:0, one launch (start us, length us, event | category | flops | bytes accessed | tf_op | source)
XLA Modules:
  0.0 179.8 jit_solution(7883190322390066773)
XLA Ops:
  6.6 2.5 %cosine_convert_fusion = (bf16[1024,64]{1,0:T(8,128)(2,1)S(1)}, bf16[1024,64]{1,0:T(8,128)(2,1)S(1)}) fusion(s32[1024]{0:T(1024)S(1)} %iota_add_fusion), kind=kLoop, calls=%fused_computation.154 | loop fusion | flops 1048576 | bytes 266240 | tf_op jit(solution)/shard_map/convert.2
  9.1 3.9 %convolution_bitcast_fusion = f32[2048,128]{0,1:T(8,128)S(1)} fusion(bf16[2048,1024]{1,0:T(8,128)(2,1)} %bitcast.232, bf16[1024,64]{1,0:T(8,128)(2,1)S(1)} %get-tuple-element.144, bf16[1024,64]{1,0:T(8,128)(2,1)S(1)} %get-tuple-element.143), kind=kOutput, calls=%fused_computation.8 | convolution fusion | flops 537395200 | bytes 5505024 | tf_op jit(solution)/shard_map/dot_general | solution.py:152
  13.0 0.9 reshape.10782
  13.9 0.8 fusion.186
  15.6 1.3 fusion.4
  17.1 1.1 sine_convert_fusion.1
  18.2 1.0 fusion.110
  20.3 0.6 fusion.187
  21.6 16.4 %all-reduce.2.cloned.1.call-done = bf16[1024,128]{1,0:T(8,128)(2,1)} async-done(((bf16[1024,128]{1,0:T(8,128)(2,1)}), bf16[1024,128]{1,0:T(8,128)(2,1)}) %all-reduce.2.cloned.1.call-update) | async-done | bytes 262160 | tf_op jit(solution)/shard_map/psum | solution.py:164
  38.0 1.7 fusion.82
  39.7 0.7 fusion.86
  40.4 1.1 fusion.50
  41.6 0.9 fusion.28
  42.4 0.9 fusion.24
  43.3 0.9 fusion.22
  44.2 1.0 fusion.32
  45.2 0.8 fusion.48
  47.3 0.6 sqrt_multiply_fusion
  48.0 0.7 rsqrt_multiply_fusion.9
  48.6 0.7 rsqrt_multiply_fusion.3
  49.3 0.7 sqrt_multiply_fusion.1
  50.4 4.1 %multiply_add_fusion = (f32[128,4,1,1024]{3,1,2,0:T(4,128)S(1)}, f32[128,4,1,1024]{3,1,2,0:T(4,128)S(1)}) fusion(f32[4,1024]{1,0:T(4,128)S(1)} %get-tuple-element.42, f32[128,1024]{1,0:T(8,128)S(1)} %get-tuple-element.103, f32[4,1024]{1,0:T(4,128)S(1)} %get-tuple-element.41, f32[128,1024]{1,0:T(8,128)S(1)} %get-tuple-element.109, ...), kind=kLoop, calls=%fused_computation.10 | loop fusion | flops 15728640 | bytes 8519680 | tf_op jit(solution)/shard_map/add | solution.py:122
  54.6 4.2 %multiply_add_fusion.1 = (f32[128,4,1,1024]{3,1,2,0:T(4,128)S(1)}, f32[128,4,1,1024]{3,1,2,0:T(4,128)S(1)}) fusion(f32[4,1024]{1,0:T(4,128)S(1)} %get-tuple-element.71, f32[128,1024]{1,0:T(8,128)S(1)} %get-tuple-element.112, f32[4,1024]{1,0:T(4,128)S(1)} %get-tuple-element.70, f32[128,1024]{1,0:T(8,128)S(1)} %get-tuple-element.114, ...), kind=kLoop, calls=%fused_computation.12 | loop fusion | flops 15728640 | bytes 8519680 | tf_op jit(solution)/shard_map/add | solution.py:122
  58.7 2.1 %fusion.1 = bf16[128,4,2,1024]{3,1,2,0:T(4,128)(2,1)S(1)} fusion(f32[128,4,1,1024]{3,1,2,0:T(4,128)S(1)} %get-tuple-element.98, f32[128,4,1,1024]{3,1,2,0:T(4,128)S(1)} %get-tuple-element.97, f32[128,4,1,1024]{3,1,2,0:T(4,128)S(1)} %get-tuple-element.96, f32[128,4,1,1024]{3,1,2,0:T(4,128)S(1)} %get-tuple-element.95, f32[128]{0:T(128)S(1)} %get-tuple-element.146, ...), kind=kLoop, calls=%fused_computation.4 | loop fusion | flops 6291456 | bytes 10486784 | tf_op jit(solution)/shard_map/convert_element_type | solution.py:186
  60.8 9.8 %gather_fusion = bf16[256,4,2,1024]{3,1,2,0:T(4,128)(2,1)} fusion(bf16[128,4,2,1024]{3,1,2,0:T(4,128)(2,1)S(1)} %fusion.1, s32[1024]{0:T(1024)S(1)} %pad_clamp_fusion.1), kind=kCustom, calls=%fused_computation | custom fusion | bytes 8389632 | tf_op jit(solution)/shard_map/jit(_take)/gather | solution.py:207
  70.7 7.1 %fusion.2 = bf16[32,8,4,2,1024]{4,1,0,3,2:T(8,128)(2,1)S(1)} fusion(bf16[256,4,2,1024]{3,1,2,0:T(4,128)(2,1)} %gather_fusion, pred[32,8]{1,0:T(8,128)(4,1)S(1)} %copy.25, bf16[32]{0:T(256)(128)(2,1)S(1)} %convert_element_type.86), kind=kLoop, calls=%fused_computation.7 | loop fusion | flops 4194304 | bytes 8388928 | tf_op jit(solution)/shard_map/mul | solution.py:210
  77.7 2.4 %copy.30 = bf16[32,8,4,2,1024]{4,1,3,2,0:T(8,128)(2,1)} copy(bf16[32,8,4,2,1024]{4,1,0,3,2:T(8,128)(2,1)S(1)} %fusion.2) | data formatting | bytes 8388608 | tf_op jit(solution)/shard_map/mul | solution.py:210
  80.5 21.9 %psum.15 = f32[128]{0:T(128)S(1)} all-reduce(f32[128]{0:T(128)S(1)} %get-tuple-element.149), channel_id=1, replica_groups=mesh['cell'=2,'ap'=8,'sc'=2] {'ap'}, use_global_device_ids=true, to_apply=%region_41.42 | all-reduce | flops 128 | bytes 1024 | tf_op jit(solution)/shard_map/psum | solution.py:179
  102.4 0.7 gather_fusion.1
  103.4 66.6 %reduce-scatter.2.cloned.1.call-done = bf16[4,8,4,2,1024]{4,1,3,2,0:T(8,128)(2,1)} async-done(((bf16[32,8,4,2,1024]{4,1,3,2,0:T(8,128)(2,1)}), bf16[4,8,4,2,1024]{4,1,3,2,0:T(8,128)(2,1)}) %reduce-scatter.2.cloned.1.call-update) | async-done | bytes 524304 | tf_op jit(solution)/shard_map/reduce_scatter | solution.py:209
  170.0 1.2 convert_divide_fusion
  171.2 1.8 copy.32
  (68 shorter events, 5.0 us)
Async XLA Ops:
  6.5 31.5 %all-reduce.2.cloned.1.call-start = ((), (), s32[]{:S(2)}) async-start(), calls=%async_computation.1 | async-start | bytes 524288 | tf_op jit(solution)/shard_map/psum | solution.py:164
  14.7 4.5 %copy-start.4 = (s32[128]{0:T(128)S(1)}, s32[128]{0:T(128)}, u32[]{:S(2)}) copy-start(s32[128]{0:T(128)} %param.13) | copy-start | bytes 1540
  14.7 4.7 %copy-start.2 = (s32[16,1]{0,1:T(1,128)S(1)}, s32[16,1]{0,1:T(1,128)}, u32[]{:S(2)}) copy-start(s32[16,1]{0,1:T(1,128)} %param.15) | copy-start | bytes 196
  14.7 5.6 %copy-start.7 = (f32[128]{0:T(128)S(1)}, f32[128]{0:T(128)}, u32[]{:S(2)}) copy-start(f32[128]{0:T(128)} %param.10) | copy-start | bytes 1540
  14.7 5.6 %copy-start.3 = (f32[2]{0:T(128)S(1)}, f32[2]{0:T(128)}, u32[]{:S(2)}) copy-start(f32[2]{0:T(128)} %param.11) | copy-start | bytes 28
  14.7 6.3 %copy-start.5 = (s32[16,16]{1,0:T(8,128)S(1)}, s32[16,16]{1,0:T(8,128)}, u32[]{:S(2)}) copy-start(s32[16,16]{1,0:T(8,128)} %param.14) | copy-start | bytes 3076
  14.7 6.3 %copy-start.6 = (f32[2,128]{1,0:T(2,128)S(1)}, f32[2,128]{1,0:T(2,128)}, u32[]{:S(2)}) copy-start(f32[2,128]{1,0:T(2,128)} %param.12) | copy-start | bytes 3076
  14.8 6.8 %copy-start.1 = (bf16[2,4,2,4,1024]{4,3,2,1,0:T(4,128)(2,1)S(1)}, bf16[2,4,2,4,1024]{4,3,2,1,0:T(4,128)(2,1)}, u32[]{:S(2)}) copy-start(bf16[2,4,2,4,1024]{4,3,2,1,0:T(4,128)(2,1)} %param.9) | copy-start | bytes 393220
  16.9 153.1 %reduce-scatter.2.cloned.1.call-start = ((), (), s32[]{:S(2)}) async-start(), calls=%async_computation.2 | async-start | bytes 4718592 | tf_op jit(solution)/shard_map/reduce_scatter | solution.py:209
  38.0 1.7 copy-start
Sparse Core Ops, SparseCore 0:
  17.0 20.9 all-reduce.1
  80.3 89.6 reduce-scatter.1
where the time goes:
time: 180 us
  waiting for transfers between devices  83.1 us (46%)
  other arithmetic  34.6 us (19%)
  blocking collectives  21.9 us (12%)
  local copies, waits for them, and re-layouts  18.4 us (10%)
  between operations  13.8 us (8%)
  matrix products  7.85 us (4%)
    reduce_scatter x1, waiting for transfers between devices, local(): lax.psum_scatter(picked * filled.astype(jnp.bfloat16)[:, None, None, None...  66.6 us
    psum x1, blocking collectives, local(): totals = lax.psum(jnp.sum(weights, axis=0), 'ap')  21.9 us
    psum x1, waiting for transfers between devices, local(): coefficients = lax.psum(combined.astype(jnp.bfloat16), 'sc')  16.4 us
    gather x1, local copies, waits for them, and re-layouts, local(): picked = jnp.take(partial_value, member_rows.reshape(-1), axis=0)  9.81 us
    add x2, other arithmetic, local_estimates(): est_re + smooth_re[i][:, None, :] * solved[i][0][None]  8.3 us
    mul x1, other arithmetic, local(): picked * filled.astype(jnp.bfloat16)[:, None, None, None, None]  7.08 us
    dot_general x1, matrix products, local(): jnp.dot(unsmoothed_link_guesses.reshape(-1, tone_positions), forward_tabl...  3.9 us
    another operation x3, other arithmetic  3.78 us
  transfers between devices with their start and end apart: 2, of which 2 were waited for; matrix products, arithmetic and copies ran while one was open for 3% of the time, Pallas kernels for 0%

commit v1 on v0

--- a/solution.py
+++ b/solution.py
@@ -176,7 +176,7 @@
         jnp.float32
     )
     weights = jnp.dot(onehot, own_columns, precision=lax.Precision.HIGHEST).T * ap_gain
-    totals = lax.psum(jnp.sum(weights, axis=0), "ap")
+    totals = jnp.sum(lax.all_gather(jnp.sum(weights, axis=0), "ap"), axis=0)
     partial_value = local_estimates(
         smooth_re[0], smooth_im[0], user_power, noise_power[0], received[0], weights[0]
     )

time: 180 us -> 180 us (level)
    psum x1 -> x0, blocking collectives: 21.9 us -> none  [local(): totals = lax.psum(jnp.sum(weights, axis=0), 'ap')]
    all_gather x0 -> x1, blocking collectives: none -> 21.2 us  [local(): totals = jnp.sum(lax.all_gather(jnp.sum(weights, axis=0), 'ap'), axis=0)]
where the time goes in v1:
time: 180 us
  waiting for transfers between devices  83.7 us (46%)
  other arithmetic  34.6 us (19%)
  blocking collectives  21.2 us (12%)
  local copies, waits for them, and re-layouts  18.4 us (10%)
  between operations  13.8 us (8%)
  matrix products  7.85 us (4%)
    reduce_scatter x1, waiting for transfers between devices, local(): lax.psum_scatter(picked * filled.astype(jnp.bfloat16)[:, None, None, None...  67.2 us
    all_gather x1, blocking collectives, local(): totals = jnp.sum(lax.all_gather(jnp.sum(weights, axis=0), 'ap'), axis=0)  21.2 us
    psum x1, waiting for transfers between devices, local(): coefficients = lax.psum(combined.astype(jnp.bfloat16), 'sc')  16.4 us
    gather x1, local copies, waits for them, and re-layouts, local(): picked = jnp.take(partial_value, member_rows.reshape(-1), axis=0)  9.81 us
    add x2, other arithmetic, local_estimates(): est_re + smooth_re[i][:, None, :] * solved[i][0][None]  8.31 us
    mul x1, other arithmetic, local(): picked * filled.astype(jnp.bfloat16)[:, None, None, None, None]  7.08 us
    dot_general x1, matrix products, local(): jnp.dot(unsmoothed_link_guesses.reshape(-1, tone_positions), forward_tabl...  3.9 us
    another operation x3, other arithmetic  3.78 us
  transfers between devices with their start and end apart: 2, of which 2 were waited for; matrix products, arithmetic and copies ran while one was open for 3% of the time, Pallas kernels for 0%

profile of v1, /device:TPU:0, one launch (start us, length us, event | category | flops | bytes accessed | tf_op | source)
XLA Modules:
  0.0 179.7 jit_solution(5470798991702730159)
XLA Ops:
  6.6 2.5 %cosine_convert_fusion = (bf16[1024,64]{1,0:T(8,128)(2,1)S(1)}, bf16[1024,64]{1,0:T(8,128)(2,1)S(1)}) fusion(s32[1024]{0:T(1024)S(1)} %iota_add_fusion), kind=kLoop, calls=%fused_computation.154 | loop fusion | flops 1048576 | bytes 266240 | tf_op jit(solution)/shard_map/convert.2
  9.1 3.9 %convolution_bitcast_fusion = f32[2048,128]{0,1:T(8,128)S(1)} fusion(bf16[2048,1024]{1,0:T(8,128)(2,1)} %bitcast.233, bf16[1024,64]{1,0:T(8,128)(2,1)S(1)} %get-tuple-element.144, bf16[1024,64]{1,0:T(8,128)(2,1)S(1)} %get-tuple-element.143), kind=kOutput, calls=%fused_computation.8 | convolution fusion | flops 537395200 | bytes 5505024 | tf_op jit(solution)/shard_map/dot_general | solution.py:152
  13.0 0.9 reshape.10782
  13.9 0.8 fusion.186
  15.6 1.3 fusion.4
  17.1 1.1 sine_convert_fusion.1
  18.2 1.0 fusion.110
  20.3 0.6 fusion.187
  21.6 16.4 %all-reduce.2.cloned.1.call-done = bf16[1024,128]{1,0:T(8,128)(2,1)} async-done(((bf16[1024,128]{1,0:T(8,128)(2,1)}), bf16[1024,128]{1,0:T(8,128)(2,1)}) %all-reduce.2.cloned.1.call-update) | async-done | bytes 262160 | tf_op jit(solution)/shard_map/psum | solution.py:164
  38.0 1.7 fusion.82
  39.7 0.7 fusion.86
  40.4 1.1 fusion.50
  41.6 0.9 fusion.28
  42.4 0.9 fusion.24
  43.3 0.9 fusion.22
  44.2 1.0 fusion.32
  45.2 0.8 fusion.48
  47.3 0.6 sqrt_multiply_fusion
  48.0 0.7 rsqrt_multiply_fusion.9
  48.6 0.7 rsqrt_multiply_fusion.3
  49.3 0.7 sqrt_multiply_fusion.1
  50.4 4.2 %multiply_add_fusion = (f32[128,4,1,1024]{3,1,2,0:T(4,128)S(1)}, f32[128,4,1,1024]{3,1,2,0:T(4,128)S(1)}) fusion(f32[4,1024]{1,0:T(4,128)S(1)} %get-tuple-element.42, f32[128,1024]{1,0:T(8,128)S(1)} %get-tuple-element.103, f32[4,1024]{1,0:T(4,128)S(1)} %get-tuple-element.41, f32[128,1024]{1,0:T(8,128)S(1)} %get-tuple-element.109, ...), kind=kLoop, calls=%fused_computation.10 | loop fusion | flops 15728640 | bytes 8519680 | tf_op jit(solution)/shard_map/add | solution.py:122
  54.6 4.2 %multiply_add_fusion.1 = (f32[128,4,1,1024]{3,1,2,0:T(4,128)S(1)}, f32[128,4,1,1024]{3,1,2,0:T(4,128)S(1)}) fusion(f32[4,1024]{1,0:T(4,128)S(1)} %get-tuple-element.71, f32[128,1024]{1,0:T(8,128)S(1)} %get-tuple-element.112, f32[4,1024]{1,0:T(4,128)S(1)} %get-tuple-element.70, f32[128,1024]{1,0:T(8,128)S(1)} %get-tuple-element.114, ...), kind=kLoop, calls=%fused_computation.12 | loop fusion | flops 15728640 | bytes 8519680 | tf_op jit(solution)/shard_map/add | solution.py:122
  58.7 2.1 %fusion.1 = bf16[128,4,2,1024]{3,1,2,0:T(4,128)(2,1)S(1)} fusion(f32[128,4,1,1024]{3,1,2,0:T(4,128)S(1)} %get-tuple-element.98, f32[128,4,1,1024]{3,1,2,0:T(4,128)S(1)} %get-tuple-element.97, f32[128,4,1,1024]{3,1,2,0:T(4,128)S(1)} %get-tuple-element.96, f32[128,4,1,1024]{3,1,2,0:T(4,128)S(1)} %get-tuple-element.95, f32[128]{0:T(128)S(1)} %get-tuple-element.146, ...), kind=kLoop, calls=%fused_computation.4 | loop fusion | flops 6291456 | bytes 10486784 | tf_op jit(solution)/shard_map/convert_element_type | solution.py:186
  60.8 9.8 %gather_fusion = bf16[256,4,2,1024]{3,1,2,0:T(4,128)(2,1)} fusion(bf16[128,4,2,1024]{3,1,2,0:T(4,128)(2,1)S(1)} %fusion.1, s32[1024]{0:T(1024)S(1)} %pad_clamp_fusion.1), kind=kCustom, calls=%fused_computation | custom fusion | bytes 8389632 | tf_op jit(solution)/shard_map/jit(_take)/gather | solution.py:207
  70.6 7.1 %fusion.2 = bf16[32,8,4,2,1024]{4,1,0,3,2:T(8,128)(2,1)S(1)} fusion(bf16[256,4,2,1024]{3,1,2,0:T(4,128)(2,1)} %gather_fusion, pred[32,8]{1,0:T(8,128)(4,1)S(1)} %copy.25, bf16[32]{0:T(256)(128)(2,1)S(1)} %convert_element_type.86), kind=kLoop, calls=%fused_computation.7 | loop fusion | flops 4194304 | bytes 8388928 | tf_op jit(solution)/shard_map/mul | solution.py:210
  77.7 2.4 %copy.30 = bf16[32,8,4,2,1024]{4,1,3,2,0:T(8,128)(2,1)} copy(bf16[32,8,4,2,1024]{4,1,0,3,2:T(8,128)(2,1)S(1)} %fusion.2) | data formatting | bytes 8388608 | tf_op jit(solution)/shard_map/mul | solution.py:210
  80.5 21.2 %all-gather.1 = f32[8,1,128]{2,1,0:T(1,128)S(1)} all-gather(f32[1,1,128]{2,1,0:T(1,128)S(1)} %bitcast.239), channel_id=2, replica_groups=mesh['cell'=2,'ap'=8,'sc'=2] {'ap'}, dimensions={0}, use_global_device_ids=true | all-gather | bytes 4608 | tf_op jit(solution)/shard_map/all_gather | solution.py:179
  101.7 0.7 gather_fusion.1
  102.7 67.2 %reduce-scatter.2.cloned.1.call-done = bf16[4,8,4,2,1024]{4,1,3,2,0:T(8,128)(2,1)} async-done(((bf16[32,8,4,2,1024]{4,1,3,2,0:T(8,128)(2,1)}), bf16[4,8,4,2,1024]{4,1,3,2,0:T(8,128)(2,1)}) %reduce-scatter.2.cloned.1.call-update) | async-done | bytes 524304 | tf_op jit(solution)/shard_map/reduce_scatter | solution.py:209
  169.9 1.2 convert_divide_fusion
  171.1 1.8 copy.32
  (69 shorter events, 5.0 us)
Async XLA Ops:
  6.5 31.5 %all-reduce.2.cloned.1.call-start = ((), (), s32[]{:S(2)}) async-start(), calls=%async_computation.1 | async-start | bytes 524288 | tf_op jit(solution)/shard_map/psum | solution.py:164
  14.7 4.5 %copy-start.4 = (s32[128]{0:T(128)S(1)}, s32[128]{0:T(128)}, u32[]{:S(2)}) copy-start(s32[128]{0:T(128)} %param.13) | copy-start | bytes 1540
  14.7 4.7 %copy-start.2 = (s32[16,1]{0,1:T(1,128)S(1)}, s32[16,1]{0,1:T(1,128)}, u32[]{:S(2)}) copy-start(s32[16,1]{0,1:T(1,128)} %param.15) | copy-start | bytes 196
  14.7 5.6 %copy-start.7 = (f32[128]{0:T(128)S(1)}, f32[128]{0:T(128)}, u32[]{:S(2)}) copy-start(f32[128]{0:T(128)} %param.10) | copy-start | bytes 1540
  14.7 5.6 %copy-start.3 = (f32[2]{0:T(128)S(1)}, f32[2]{0:T(128)}, u32[]{:S(2)}) copy-start(f32[2]{0:T(128)} %param.11) | copy-start | bytes 28
  14.7 6.3 %copy-start.5 = (s32[16,16]{1,0:T(8,128)S(1)}, s32[16,16]{1,0:T(8,128)}, u32[]{:S(2)}) copy-start(s32[16,16]{1,0:T(8,128)} %param.14) | copy-start | bytes 3076
  14.7 6.3 %copy-start.6 = (f32[2,128]{1,0:T(2,128)S(1)}, f32[2,128]{1,0:T(2,128)}, u32[]{:S(2)}) copy-start(f32[2,128]{1,0:T(2,128)} %param.12) | copy-start | bytes 3076
  14.8 6.8 %copy-start.1 = (bf16[2,4,2,4,1024]{4,3,2,1,0:T(4,128)(2,1)S(1)}, bf16[2,4,2,4,1024]{4,3,2,1,0:T(4,128)(2,1)}, u32[]{:S(2)}) copy-start(bf16[2,4,2,4,1024]{4,3,2,1,0:T(4,128)(2,1)} %param.9) | copy-start | bytes 393220
  16.9 153.0 %reduce-scatter.2.cloned.1.call-start = ((), (), s32[]{:S(2)}) async-start(), calls=%async_computation.2 | async-start | bytes 4718592 | tf_op jit(solution)/shard_map/reduce_scatter | solution.py:209
  38.0 1.7 copy-start
Sparse Core Ops, SparseCore 0:
  17.0 20.9 all-reduce.1
  80.3 89.5 reduce-scatter.1
